TPU v7x, 32 devices: a whole 2x2x4 slice. The times are simulated.
32 devices in a mesh: expert: 8 (over z, y), tensor: 4 (over x, core).
Axes of the slice: x: 2, y: 2, z: 4, core: 2. Of those that a mesh axis runs over, the one named last changes fastest.
Arguments:
- inputs: bfloat16 [12608, 512], P('expert'), may hold values from -6 to 6
- gain_attend: float32 [512], replicated, may hold values from 0.25 to 1.75
- triple_weight: bfloat16 [512, 3, 512], P(None, None, 'tensor'), may hold values from -0.25 to 0.25
- project_weight: bfloat16 [512, 512], P('tensor'), may hold values from -1.5 to 1.5
- gain_mixture: float32 [512], replicated, may hold values from 0.25 to 1.75
- router_weight: bfloat16 [512, 16], replicated, may hold values from -0.125 to 0.125
- expert_first: bfloat16 [16, 512, 2048], P('expert', None, 'tensor'), may hold values from -0.25 to 0.25
- expert_second: bfloat16 [16, 2048, 512], P('expert', 'tensor'), may hold values from -0.1875 to 0.1875
- triple_down: bfloat16 [512, 128], replicated, may hold values from -0.25 to 0.25
- triple_up: bfloat16 [128, 3, 512], P(None, None, 'tensor'), may hold values from -1.5 to 1.5
- project_down: bfloat16 [512, 128], P('tensor'), may hold values from -1.5 to 1.5
- project_up: bfloat16 [128, 512], replicated, may hold values from -1.5 to 1.5
- router_down: bfloat16 [512, 128], replicated, may hold values from -0.25 to 0.25
- router_up: bfloat16 [128, 16], replicated, may hold values from -0.75 to 0.75
- first_down: bfloat16 [512, 128], replicated, may hold values from -0.25 to 0.25
- first_up: bfloat16 [128, 2048], P(None, 'tensor'), may hold values from -1.5 to 1.5
- second_down: bfloat16 [2048, 128], P('tensor'), may hold values from -0.1875 to 0.1875
- second_up: bfloat16 [128, 512], replicated, may hold values from -1.5 to 1.5
- adapter_index: int32 [64], P('expert'), may hold values from 0 to 7
- routes: int32 [12608, 2], P('expert'), may hold values from 0 to 15, all different within a row
- priority: int32 [8, 1576], P('expert'), may hold values from 0 to 1575, each once within a row
- cotangent: bfloat16 [12608, 512], P('expert'), may hold values from -6 to 6
Outputs:
- block_output: bfloat16 [12608, 512], P('expert')
- input_grad: bfloat16 [12608, 512], P('expert')
- triple_down_grad: float32 [512, 128], replicated
- triple_up_grad: float32 [128, 3, 512], P(None, None, 'tensor')
- project_down_grad: float32 [512, 128], P('tensor')
- project_up_grad: float32 [128, 512], replicated
- router_down_grad: float32 [512, 128], replicated
- router_up_grad: float32 [128, 16], replicated
- first_down_grad: float32 [512, 128], replicated
- first_up_grad: float32 [128, 2048], P(None, 'tensor')
- second_down_grad: float32 [2048, 128], P('tensor')
- second_up_grad: float32 [128, 512], replicated
Inputs may be any that keep to these rules, and one draw needn't show every extreme that they name: `routes`: each row names 2 different experts. `priority`: each row holds every token index of its group once.
All inputs are finite; a program needn't handle non-finite values.
Results may differ from a plain program's by a relative error of at most 0.028.
Values may be sent and summed in bfloat16 or wider, within the bound.
A program may use at most 192 MiB of HBM per device.

v0:
```python
import functools

import jax
import jax.numpy as jnp
from jax import lax
from jax.experimental import pallas as pl
from jax.experimental.pallas import tpu as pltpu
from jax.sharding import PartitionSpec as P

HEAD_DIM = 64
TOP = 2
ADAPTERS = 8
RANK = 16
ADAPT = ADAPTERS * RANK
EPS = 1e-06

f32 = jnp.float32
bf16 = jnp.bfloat16
i32 = jnp.int32
MESH = pl.DeviceIdType.MESH
VMEM = pltpu.VMEM


def up(a, b):
    return -(-a // b) * b


def dot(a, b):
    return lax.dot_general(a, b, (((1,), (0,)), ((), ())), preferred_element_type=f32)


def dot_nt(a, b):
    return lax.dot_general(a, b, (((1,), (1,)), ((), ())), preferred_element_type=f32)


def dot_tn(a, b):
    return lax.dot_general(a, b, (((0,), (0,)), ((), ())), preferred_element_type=f32)


def split_high_low(a):
    high = a.astype(bf16)
    return high, (a - high.astype(f32)).astype(bf16)


def dot_fine(a, b):
    high, low = split_high_low(a)
    return dot(high, b) + dot(low, b)


def dot_nt_fine(a, b):
    high, low = split_high_low(a)
    return dot_nt(high, b) + dot_nt(low, b)


def iota(shape, axis):
    return lax.broadcasted_iota(i32, shape, axis)


def to_row(col):
    n = col.shape[0]
    return jnp.sum(jnp.where(iota((n, n), 0) == iota((n, n), 1), col, 0.0), axis=0, keepdims=True)


def to_col(row):
    n = row.shape[1]
    return jnp.sum(jnp.where(iota((n, n), 0) == iota((n, n), 1), row, 0.0), axis=1, keepdims=True)


def picks_of(adapters, base, per, seqp):
    lane = iota((seqp, ADAPT), 1) // RANK
    return jnp.concatenate(
        [(lane == adapters[base + li]).astype(f32) for li in range(per)], axis=0
    )


def whole(count):
    return [pl.BlockSpec(memory_space=VMEM) for _ in range(count)]


def norm_stats(x):
    centre = jnp.mean(x, axis=-1, keepdims=True)
    shifted = x - centre
    scale = lax.rsqrt(jnp.mean(shifted * shifted, axis=-1, keepdims=True) + EPS)
    return shifted * scale, scale


def norm_back(grad, gain, unit, scale):
    g = grad * gain
    return scale * (
        g - jnp.mean(g, axis=-1, keepdims=True) - unit * jnp.mean(g * unit, axis=-1, keepdims=True)
    )


def greet(peers):
    barrier = pltpu.get_barrier_semaphore()
    for peer in peers:
        pl.semaphore_signal(barrier, 1, device_id=peer, device_id_type=MESH)
    pl.semaphore_wait(barrier, len(peers))


def remote(src, dst, send, recv, peer):
    return pltpu.make_async_remote_copy(
        src_ref=src, dst_ref=dst, send_sem=send, recv_sem=recv, device_id=peer, device_id_type=MESH
    )


def where_am_i():
    e = lax.axis_index("expert")
    t = lax.axis_index("tensor")
    return e, t, jnp.bitwise_xor(t, 1), jnp.bitwise_xor(t, 2), jnp.bitwise_xor(t, 3)


def dma(n):
    return pltpu.SemaphoreType.DMA((n,))


def linked(ident):
    return pltpu.CompilerParams(collective_id=ident, has_side_effects=True)


def gates_of(mixed, r0, r1, pick, rw, rd, ru):
    low = dot(mixed, rd) * pick
    logits = dot_nt(mixed, rw) + dot_nt_fine(low, ru)
    lane = iota((1, rw.shape[0]), 1)
    first = jnp.sum(jnp.where(r0 == lane, logits, 0.0), axis=1, keepdims=True)
    second = jnp.sum(jnp.where(r1 == lane, logits, 0.0), axis=1, keepdims=True)
    top = jnp.maximum(first, second)
    a = jnp.exp(first - top)
    b = jnp.exp(second - top)
    return a / (a + b), b / (a + b), low


def own_images(ref, first, per, seq, seqp, put):
    tok = ref.shape[0]
    for li in range(per):
        row = iota((seqp, tok), 0)
        sel = (iota((seqp, tok), 1) == row + (first + li) * seq) & (row < seq)
        put(pl.ds(li * seqp, seqp), dot(sel.astype(f32).astype(bf16), ref[...]))


def erf_parts(pre):
    cdf = 0.5 * (1.0 + lax.erf(pre * 0.7071067811865476))
    return pre * cdf, cdf + pre * (jnp.exp(-0.5 * pre * pre) * 0.3989422804014327)


def chunk_of(ref, ne, p):
    size = ref.shape[0] // ne
    return pl.ds(pl.multiple_of(p * size, size), size)


def sum_copy(ne, src, parts, send, recv):
    e, t = where_am_i()[:2]

    def copy(d):
        p = lax.rem(e + d, ne)
        return remote(src.at[chunk_of(src, ne, p)], parts.at[d - 1], send.at[d], recv.at[d], (p, t))

    return copy


def start_all(ne, copy):
    def start(d, carry):
        copy(d).start()
        return carry

    lax.fori_loop(1, ne, start, 0)


def sum_share(ne, copy, src, parts, total, send, recv):
    e, t = where_am_i()[:2]
    mine = chunk_of(src, ne, e)

    def add(d, acc):
        copy(d).wait()
        return acc + parts[d - 1].astype(f32)

    total[mine, :] = lax.fori_loop(1, ne, add, src[mine, :].astype(f32)).astype(bf16)

    def share(d):
        p = lax.rem(e + d, ne)
        return remote(total.at[mine], total.at[mine], send.at[ne + d], recv.at[ne + d], (p, t))

    def start(d, carry):
        share(d).start()
        return carry

    lax.fori_loop(1, ne, start, 0)
    return share


def wait_all(ne, copy):
    def wait(d, carry):
        copy(d).wait()
        return carry

    lax.fori_loop(1, ne, wait, 0)


def block_kernel(
    dims, adapters, prio, routes, cot_in, x_in, gain1, gain2, wt_in, tup_in, pw_in, pd_in,
    tdn, pup, rw, rd, ru, fdn, sup, w1_in, w2_in, fup_in, sdn_in,
    etot, btot, atot, outs, rep_e, rep_a, back_out, res_out, *rest,
):
    nt, ne, seq, seqp, images, experts, cap, chunks, cp, held_e, grows, la, lb, roomy = dims
    (
        slotc, slotr, routec, xs, cot_own, mixed, middle, triple, attended, tlow, plow, attn_in,
        wt, tup, pw, pd, got, got_cot, cot_pad, one_s, cots, mall, gall, acc_s, gate_s, out_s,
        w1, w2, fup, sdn, sent_s, sg_s, low_s, gcol_s, gg_rows, acc_low,
        acc_fd, acc_fu, acc_sd, acc_su, gr_s, gin1, keep, gin2, cot, x_own,
        back_s, res_s, tin1, tin1k, tin1r, keep_g, keep_k, tin2, tin2k, tin2r,
        bin1, bin2, ain1, ain2, eparts, bparts, aparts, gt_s, ga_s, back_low, rank_r,
        wsend, wrecv, bsend, brecv, csend, crecv, tsend, trecv, send, recv, gsend, grecv, rsend, rrecv,
        ssend, srecv, usend, urecv, esend, erecv, b2send, b2recv, asend, arecv, osend, orecv,
        here, own_sem, load_sem, ret_sem,
    ) = rest
    back = back_s if roomy else back_out
    ebuf, bbuf = gin1.at[0], bin1.at[0]
    got_res = res_s if roomy else res_out
    e, t, near, far, cross = where_am_i()
    lw = pw_in.shape[0]
    width = x_in.shape[1]
    local = w1_in.shape[0]
    parts = nt // local
    n_out, block = cots.shape[0], cots.shape[1]
    peers = [(e, far), (e, near)] + [(lax.rem(e + d, ne), t) for d in range(1, ne)]
    barrier = pltpu.get_barrier_semaphore()
    for peer in peers:
        pl.semaphore_signal(barrier, 1, device_id=peer, device_id_type=MESH)

    def big_ref(k, to):
        return (fup_in, sdn_in)[k] if k < 2 else (w1_in, w2_in)[k - 2].at[lax.div(to, parts)]

    big = (fup, sdn, w1, w2)
    n_big = len(big)
    big_own = [
        pltpu.make_async_copy(big_ref(k, t), big[k].at[t], load_sem.at[k]) for k in range(n_big)
    ]
    big_far = [
        remote(big_ref(k, far), big[k].at[t], bsend.at[3 * k], brecv.at[3 * k], (e, far))
        for k in range(n_big)
    ]
    big_near = [
        remote(big_ref(k, near), big[k].at[t], bsend.at[3 * k + 1], brecv.at[3 * k + 1], (e, near))
        for k in range(n_big)
    ]
    big_relay = [
        remote(big[k].at[far], big[k].at[far], bsend.at[3 * k + 2], brecv.at[3 * k + 2], (e, near))
        for k in range(n_big)
    ]
    load_cot = pltpu.make_async_copy(cot_in, cot, load_sem.at[n_big])
    x_ref = x_own if roomy else cot
    load_x = pltpu.make_async_copy(x_in, x_ref, load_sem.at[n_big + 1])
    for copy in [load_cot] + big_own:
        copy.start()
    if roomy:
        load_x.start()

    moves = []
    for c in range(3):
        lanes = pl.ds(c * lw, lw)
        moves.append((wt_in.at[c], lambda q, lanes=lanes: wt.at[q, :, lanes]))
        moves.append((tup_in.at[c], lambda q, lanes=lanes: tup.at[q, :, lanes]))
    moves.append((pw_in, lambda q: pw.at[q]))
    moves.append((pd_in, lambda q: pd.at[q]))
    n_w = len(moves)
    fars = [
        remote(src, at(t), wsend.at[3 * i], wrecv.at[3 * i], (e, far))
        for i, (src, at) in enumerate(moves)
    ]
    nears = [
        remote(src, at(t), wsend.at[3 * i + 1], wrecv.at[3 * i + 1], (e, near))
        for i, (src, at) in enumerate(moves)
    ]
    relays = [
        remote(at(far), at(far), wsend.at[3 * i + 2], wrecv.at[3 * i + 2], (e, near))
        for i, (src, at) in enumerate(moves)
    ]
    owns = [
        pltpu.make_async_copy(src, at(t), own_sem.at[i]) for i, (src, at) in enumerate(moves)
    ]
    for copy in owns:
        copy.start()

    tok = prio.shape[1]
    per = images // nt
    rows = per * seqp
    total = nt * rows
    wide = one_s.shape[-1]
    order = iota((seqp, tok), 1).astype(f32)
    lane = iota((seqp, wide), 1)
    for i in range(images):
        if i == images // 2:
            pl.semaphore_wait(barrier, len(peers))
            for copy in fars + nears:
                copy.start()
        q, at = i // per, pl.ds(i % per * seqp, seqp)
        all_at = pl.ds(i * seqp, seqp)
        token = iota((seqp, 1), 0) + i * seq
        gate_s[all_at, :] = jnp.sum(
            jnp.where(prio[...] == token, order, 0.0), axis=1, keepdims=True
        )
        lane0 = i * seq // 128 * 128
        lane1 = min(lane0 + up(seq + 128, 128), tok)
        here_i = (iota((seqp, lane1 - lane0), 1) + lane0 == token) & (iota((seqp, lane1 - lane0), 0) < seq)
        r = [
            jnp.sum(
                jnp.where(here_i, routes[k : k + 1, lane0:lane1].astype(f32) + 1.0, 0.0),
                axis=1,
                keepdims=True,
            ).astype(i32)
            - 1
            for k in range(TOP)
        ]
        for k in range(TOP):
            routec[q, at, k : k + 1] = r[k]
        named = jnp.where(lane < experts, r[0], jnp.where(r[1] < 0, -1, r[1] + experts))
        one_s[all_at, :] = (named == lane).astype(f32).astype(bf16)
    totals = dot(jnp.ones((8, total), bf16), one_s[...])[0:1]
    for q in range(nt):
        rank_r[q : q + 1, :] = to_row(gate_s[pl.ds(q * rows, rows), :])
    lane = iota((rows, wide), 1)

    def slots_of(q, carry):
        at = pl.ds(pl.multiple_of(q * rows, 16), rows)
        mine = gate_s[at, :]
        counts = jnp.zeros((rows, wide), f32)
        for p in range(nt):
            before = (rank_r[p : p + 1, :] < mine).astype(f32).astype(bf16)
            counts = counts + dot(before, one_s[pl.ds(p * rows, rows), :])
        hot = one_s[at, :].astype(f32) * counts
        first = jnp.sum(jnp.where(lane < experts, hot, 0.0), axis=1, keepdims=True)
        second = jnp.sum(
            jnp.where(lane < experts, 0.0, hot)
            + jnp.where((lane < experts) & (routec[q, :, 1:2] == lane), totals, 0.0),
            axis=1,
            keepdims=True,
        )
        for k, pos in ((0, first), (1, second)):
            named = routec[q, :, k : k + 1]
            place = pos.astype(i32)
            kept = (named >= 0) & (place < cap)
            kept = kept & (lax.rem(named, local) == lax.div(t, parts))
            kept = kept & (lax.rem(place, parts) == lax.rem(t, parts))
            index = lax.div(place, parts)
            index = jnp.where(index < cp - 2, index, index + 2)
            slot = jnp.where(kept, lax.div(named, local) * block + index, -1)
            slotc[q, :, k : k + 1] = slot
            slotr[q, k : k + 1, :] = to_row(slot.astype(f32)).astype(i32)
        return carry

    lax.fori_loop(0, nt, slots_of, 0)

    load_cot.wait()
    for i in range(images):
        start = i * seq // 16 * 16
        stop = min(start + up(seq, 16) + 16, tok)
        src = iota((seqp, stop - start), 1) + start
        row = iota((seqp, stop - start), 0)
        sel = ((src == row + i * seq) & (row < seq)).astype(f32).astype(bf16)
        cot_pad[i // per, pl.ds(i % per * seqp, seqp), :] = dot(sel, cot[start:stop, :]).astype(bf16)
    step = max(1, 512 // block)
    image_of = iota((1, rows), 1) // seqp

    def pack(d, carry):
        s = iota((step * block, 1), 0) + d * (step * block)
        acc = jnp.zeros((step * block, width), f32)
        idc = jnp.zeros((step * block, 1), f32)
        for q in range(nt):
            ids = jnp.zeros((1, rows), f32)
            for li in range(per):
                ids = jnp.where(image_of == li, adapters[q * per + li].astype(f32), ids)
            g = (slotr[q, 0:1, :] == s) | (slotr[q, 1:2, :] == s)
            idc = idc + jnp.sum(jnp.where(g, ids, 0.0), axis=1, keepdims=True)
            acc = acc + dot(g.astype(f32).astype(bf16), cot_pad[q])
        row = iota((block, block), 0)
        for b in range(step):
            part = acc[b * block : (b + 1) * block]
            idr = to_row(idc[b * block : (b + 1) * block])
            head = jnp.where(row == cp - 2, idr, part[:, 0:block])
            cots[d * step + b, :, 0:block] = head.astype(bf16)
            cots[d * step + b, :, block:] = part[:, block:].astype(bf16)
        return carry

    lax.fori_loop(0, n_out // step, pack, 0)

    def cot_copy(d):
        p = lax.rem(e + d, ne)
        return remote(cots.at[p], got_cot.at[e], csend.at[d], crecv.at[d], (p, t))

    def cot_start(d, carry):
        cot_copy(d).start()
        return carry

    lax.fori_loop(1, ne, cot_start, 0)
    own_cot = pltpu.make_async_copy(cots.at[e], got_cot.at[e], here.at[0])
    own_cot.start()

    def put_x(at, value):
        xs[at, :] = value

    def put_cot(at, value):
        cot_own[at, :] = value.astype(bf16)

    if not roomy:
        own_images(cot, t * per, per, seq, seqp, put_cot)
        load_x.start()
    load_x.wait()
    own_images(x_ref, t * per, per, seq, seqp, put_x)
    pick = picks_of(adapters, t * per, per, seqp)
    unit, _ = norm_stats(xs[...])
    normed = (unit * gain1[...]).astype(bf16)
    attn_in[...] = normed
    low = (dot(normed, tdn[...]) * pick).astype(bf16)
    tlow[...] = low
    head_of = iota((1, lw), 1) // HEAD_DIM
    key_ok = iota((1, seqp), 1) < seq

    def piece(m, carry):
        p = jnp.bitwise_xor(t, m)

        @pl.when(m == 0)
        def _():
            for copy in owns:
                copy.wait()

        @pl.when(m == 1)
        def _():
            for copy in nears:
                copy.wait()

        @pl.when(m == 2)
        def _():
            for i in range(6):
                fars[i].wait_recv()
                relays[i].start()

        @pl.when(m == 3)
        def _():
            for i in range(6):
                relays[i].wait_recv()

        triple[p] = (dot(attn_in[...], wt[p]) + dot(tlow[...], tup[p])).astype(bf16)
        for li in range(per):
            at = pl.ds(li * seqp, seqp)
            q = triple[p, at, 0:lw]
            k = triple[p, at, lw : 2 * lw]
            v = triple[p, at, 2 * lw : 3 * lw]
            acc = jnp.zeros((seqp, lw), f32)
            for h in range(lw // HEAD_DIM):
                on = head_of == h
                s = dot_nt(jnp.where(on, q, 0.0).astype(bf16), k) * HEAD_DIM**-0.5
                s = jnp.where(key_ok, s, -jnp.inf)
                ex = jnp.exp(s - jnp.max(s, axis=1, keepdims=True))
                probs = (ex / jnp.sum(ex, axis=1, keepdims=True)).astype(bf16)
                acc = acc + dot(probs, jnp.where(on, v, 0.0).astype(bf16))
            attended[p, at, :] = acc.astype(bf16)
        return carry

    lax.fori_loop(0, nt, piece, 0)
    for copy in big_near:
        copy.start()
    for i in range(6, n_w):
        fars[i].wait_recv()
        relays[i].start()
    for i in range(6, n_w):
        relays[i].wait_recv()
    psum = jnp.zeros((rows, ADAPT), f32)
    branch = jnp.zeros((rows, width), f32)
    for p in range(nt):
        psum = psum + dot(attended[p], pd[p])
        branch = branch + dot(attended[p], pw[p])
    low2 = (psum * pick).astype(bf16)
    plow[...] = low2
    mid = xs[...] + branch + dot(low2, pup[...])
    middle[...] = mid
    unit2, _ = norm_stats(mid)
    mix = (unit2 * gain2[...]).astype(bf16)
    mixed[...] = mix
    mall[t] = mix

    mix_far = [
        remote(buf.at[t], buf.at[t], tsend.at[i], trecv.at[i], (e, far))
        for i, buf in enumerate((mall, gall))
    ]
    mix_near = [
        remote(buf.at[t], buf.at[t], tsend.at[2 + i], trecv.at[2 + i], (e, near))
        for i, buf in enumerate((mall, gall))
    ]
    mix_relay = [
        remote(buf.at[far], buf.at[far], tsend.at[4 + i], trecv.at[4 + i], (e, near))
        for i, buf in enumerate((mall, gall))
    ]
    mix_far[0].start()
    mix_near[0].start()
    r = routec[t]
    a, b, _ = gates_of(mix, r[:, 0:1], r[:, 1:2], pick, rw[...], rd[...], ru[...])
    gall[t] = jnp.zeros(gall.shape[1:], f32)
    gall[t, 0:1, :] = to_row(a)
    gall[t, 1:2, :] = to_row(b)
    for copy in [mix_far[1], mix_near[1]] + big_far:
        copy.start()
    step = max(1, 512 // block)

    def gather_rows(q, s):
        g0 = slotr[q, 0:1, :] == s
        g1 = slotr[q, 1:2, :] == s
        gate = jnp.sum(
            jnp.where(g0, gall[q, 0:1, :], jnp.where(g1, gall[q, 1:2, :], 0.0)), axis=1, keepdims=True
        )
        return dot((g0 | g1).astype(f32).astype(bf16), mall[q]), gate

    def add_quarter(q, fresh):
        def some(d, carry):
            at = pl.ds(pl.multiple_of(d * (step * block), step * block), step * block)
            s = iota((step * block, 1), 0) + d * (step * block)
            part, gate = gather_rows(q, s)
            acc_s[at, :] = part if fresh else acc_s[at, :] + part
            gate_s[at, :] = gate if fresh else gate_s[at, :] + gate
            return carry

        lax.fori_loop(0, n_out // step, some, 0)

    add_quarter(t, True)
    for copy in mix_near:
        copy.wait_recv()
    add_quarter(near, False)
    if roomy:
        own_images(cot, t * per, per, seq, seqp, put_cot)
    for copy in mix_far:
        copy.wait_recv()
    for copy in mix_relay:
        copy.start()
    add_quarter(far, False)
    for copy in mix_relay:
        copy.wait_recv()

    def finish(p):
        at = pl.ds(pl.multiple_of(p * block, block), block)
        part, gate = gather_rows(cross, iota((block, 1), 0) + p * block)
        part = acc_s[at, :] + part
        gate = to_row(gate_s[at, :] + gate)
        high = gate.astype(bf16).astype(f32)
        row = iota((block, block), 0)
        head = jnp.where(row == cp - 2, high, part[:, 0:block])
        head = jnp.where(row == cp - 1, gate - high, head)
        return head.astype(bf16), part[:, block:].astype(bf16)

    def chunk(h):
        return pl.ds(pl.multiple_of(h * cp, cp), cp)

    def out_copy(d, h):
        p = lax.rem(e + d, ne)
        k = d * chunks + h
        return remote(out_s.at[p, chunk(h)], got.at[e, chunk(h)], send.at[k], recv.at[k], (p, t))

    def send_one(d, carry):
        p = lax.rem(e + d, ne)
        head, tail = finish(p)
        out_s[p, :, 0:block] = head
        out_s[p, :, block:] = tail
        out_copy(d, 0).start()
        return carry

    lax.fori_loop(1, ne, send_one, 0)

    for h in range(1, chunks):

        def send_more(d, carry, h=h):
            out_copy(d, h).start()
            return carry

        lax.fori_loop(1, ne, send_more, 0)
    head, tail = finish(e)
    got[e, :, 0:block] = head
    got[e, :, block:] = tail

    n = ne
    erows = n * cp
    row_at = lax.rem(iota((erows, 1), 0), cp)
    res_at, gsent_at = pl.ds(0, erows), pl.ds(erows, erows)
    for buf in (acc_fd, acc_fu, acc_sd, acc_su):
        buf[...] = jnp.zeros_like(buf)
    for copy in big_own + big_near:
        copy.wait()

    def cot_wait(d, carry):
        cot_copy(d).wait()
        return carry

    lax.fori_loop(1, ne, cot_wait, 0)
    own_cot.wait()

    def grad_copy(d, h):
        p = lax.rem(e + d, ne)
        k = d * chunks + h
        return remote(cots.at[p, chunk(h)], back.at[e, chunk(h)], gsend.at[k], grecv.at[k], (p, t))

    def res_copy(d):
        p = lax.rem(e + d, ne)
        return remote(out_s.at[p], got_res.at[e], rsend.at[d], rrecv.at[d], (p, t))

    def experts_chunk(h, carry):
        at = chunk(h)

        def rows_wait(d, carry):
            out_copy(d, h).wait_recv()
            return carry

        lax.fori_loop(1, ne, rows_wait, 0)

        @pl.when(h == 0)
        def _():
            diag = iota((block, block), 0) == iota((block, block), 1)

            def headers(m, carry):
                idr = got_cot[m, cp - 2 : cp - 1, 0:block].astype(f32)
                gr = got[m, cp - 2 : cp - 1, 0:block].astype(f32) + got[
                    m, cp - 1 : cp, 0:block
                ].astype(f32)
                gcol_s[m, :, 0:1] = jnp.sum(jnp.where(diag, idr, 0.0), axis=1, keepdims=True)
                gcol_s[m, :, 1:2] = jnp.sum(jnp.where(diag, gr, 0.0), axis=1, keepdims=True)
                return carry

            lax.fori_loop(0, n, headers, 0)

        spare = jnp.where((h == 0) | (h == chunks - 1), cp - 2, cp)
        real = row_at < spare
        cols = gcol_s[:, at, :].reshape(erows, 2)
        sent = jnp.where(real, got[:, at, :].reshape(erows, width).astype(f32), 0.0).astype(bf16)
        cotf = jnp.where(real, got_cot[:, at, :].reshape(erows, width).astype(f32), 0.0)
        pick_e = (cols[:, 0:1] == (iota((1, ADAPT), 1) // RANK).astype(f32)).astype(f32)
        sent_s[...] = sent
        sgrad = (cols[:, 1:2] * cotf).astype(bf16)
        sg_s[...] = sgrad
        low_s[0] = (dot(sent, fdn[...]) * pick_e).astype(bf16)
        low_s[1] = (dot_nt(sgrad, sup[...]) * pick_e).astype(bf16)
        acc_low[...] = jnp.zeros_like(acc_low)
        acc_s[pl.ds(0, 2 * erows), :] = jnp.zeros((2 * erows, width), f32)

        def through(m, carry):
            c = jnp.bitwise_xor(t, m)

            @pl.when((h == 0) & (m == 2))
            def _():
                for far_copy, relay in zip(big_far, big_relay):
                    far_copy.wait_recv()
                    relay.start()

            @pl.when((h == 0) & (m == 3))
            def _():
                for relay in big_relay:
                    relay.wait_recv()

            span = min(erows, 512)
            for r0 in range(0, erows, span):
                rs = slice(r0, r0 + span)
                gs = slice(erows + r0, erows + r0 + span)
                pre = dot(sent_s[rs, :], w1[c]) + dot(low_s[0, rs, :], fup[c])
                act, slope = erf_parts(pre)
                hid = act.astype(bf16)
                acc_low[0, rs, :] += dot(hid, sdn[c])
                acc_s[rs, :] += dot(hid, w2[c])
                ghid = dot_nt(sg_s[rs, :], w2[c]) + dot_nt(low_s[1, rs, :], sdn[c])
                gpre = (ghid * slope).astype(bf16)
                acc_fu[c] += dot_tn(low_s[0, rs, :], gpre)
                acc_sd[c] += dot_tn(low_s[1, rs, :], hid)
                acc_low[1, rs, :] += dot_nt(gpre, fup[c])
                acc_s[gs, :] += dot_nt(gpre, w1[c])
            return carry

        lax.fori_loop(0, nt, through, 0)

        def sent_wait(d, carry):
            out_copy(d, h).wait_send()
            return carry

        lax.fori_loop(1, ne, sent_wait, 0)
        cols = gcol_s[:, at, :].reshape(erows, 2)
        pick_e = (cols[:, 0:1] == (iota((1, ADAPT), 1) // RANK).astype(f32)).astype(f32)
        second_low = (acc_low[0] * pick_e).astype(bf16)
        res = (acc_s[res_at, :] + dot(second_low, sup[...])).astype(bf16).astype(f32)
        cotf = got_cot[:, at, :].reshape(erows, width).astype(f32)
        acc_low[0, :, 0:1] = jnp.sum(res * cotf, axis=1, keepdims=True)
        g1low = (acc_low[1] * pick_e).astype(bf16)
        gsent = acc_s[gsent_at, :] + dot_nt(g1low, fdn[...])
        cots[:, at, :] = gsent.astype(bf16).reshape(n, cp, width)
        diag = iota((cp, block), 0) + h * cp == iota((cp, block), 1)

        def footers(m, carry):
            gg = jnp.sum(
                jnp.where(diag, acc_low[0, pl.ds(pl.multiple_of(m * cp, cp), cp), 0:1], 0.0),
                axis=0,
                keepdims=True,
            )
            total = jnp.where(h == 0, gg, gg_rows[pl.ds(m, 1), :] + gg)
            gg_rows[pl.ds(m, 1), :] = total

            @pl.when(h == chunks - 1)
            def _():
                high = total.astype(bf16).astype(f32)
                row = iota((16, block), 0)
                to = pl.ds(block - 16, 16)
                old = cots[m, to, 0:block].astype(f32)
                old = jnp.where(row == 14, high, jnp.where(row == 15, total - high, old))
                cots[m, to, 0:block] = old.astype(bf16)

            return carry

        lax.fori_loop(0, n, footers, 0)

        def grad_start(d, carry):
            grad_copy(d, h).start()
            return carry

        lax.fori_loop(1, ne, grad_start, 0)
        out_s[:, at, :] = (cols[:, 1:2] * res).astype(bf16).reshape(n, cp, width)
        acc_su[...] += dot_tn(second_low, sg_s[...])
        acc_fd[...] += dot_tn(g1low, sent_s[...])
        return carry

    gg_rows[...] = jnp.zeros_like(gg_rows)
    lax.fori_loop(0, chunks, experts_chunk, 0)
    locals_ = [
        pltpu.make_async_copy(cots.at[e], back.at[e], ret_sem.at[0]),
        pltpu.make_async_copy(out_s.at[e], got_res.at[e], ret_sem.at[1]),
    ]
    for copy in locals_:
        copy.start()

    def res_start(d, carry):
        res_copy(d).start()
        return carry

    ffq = w1.shape[2]
    quarter = width // nt
    share = ADAPT // nt
    for q in range(nt):
        off = 0
        for c in range(ffq // 128):
            gr_s[q, off : off + 128, :] = acc_fu[q, :, c * 128 : (c + 1) * 128].astype(bf16)
            off += 128
        gr_s[q, off : off + ffq, :] = acc_sd[q].T.astype(bf16)
        off += ffq
        gr_s[q, off : off + quarter, :] = acc_fd[:, q * quarter : (q + 1) * quarter].T.astype(bf16)
        off += quarter
        for c in range(width // 128):
            at = slice(q * share, (q + 1) * share)
            gr_s[q, off : off + share, :] = acc_su[at, c * 128 : (c + 1) * 128].astype(bf16)
            off += share
        if off < grows:
            gr_s[q, off:grows, :] = jnp.zeros((grows - off, 128), bf16)

    def tensor_sum(rows_at, in1, in2, k):
        a = remote(gr_s.at[cross, rows_at], in1.at[0], ssend.at[k], srecv.at[k], (e, near))
        b = remote(gr_s.at[near, rows_at], in1.at[1], ssend.at[k + 1], srecv.at[k + 1], (e, near))
        held = keep.at[rows_at]
        c = remote(held, in2, ssend.at[k + 2], srecv.at[k + 2], (e, far))

        def start():
            a.start()
            b.start()

        def cross_over():
            a.wait()
            held[...] = (gr_s[far, rows_at, :].astype(f32) + in1[0].astype(f32)).astype(bf16)
            c.start()

        def result():
            b.wait()
            c.wait()
            mine = gr_s[t, rows_at, :].astype(f32) + in1[1].astype(f32)
            return (mine + in2[...].astype(f32)).astype(bf16)

        return start, cross_over, result

    g_start, g_cross, g_result = tensor_sum(pl.ds(0, grows), gin1, gin2, 0)
    g_start()

    r = routec[t]
    prob0, prob1, rlow = gates_of(
        mixed[...], r[:, 0:1], r[:, 1:2], pick, rw[...], rd[...], ru[...]
    )
    g_cross()

    def softmax_of(qm, k):
        s = jnp.where(key_ok, dot_nt(qm, k) * HEAD_DIM**-0.5, -jnp.inf)
        ex = jnp.exp(s - jnp.max(s, axis=1, keepdims=True))
        return ex / jnp.sum(ex, axis=1, keepdims=True)

    def back_wait(d, carry):
        for h in range(chunks):
            grad_copy(d, h).wait()
        return carry

    lax.fori_loop(1, ne, back_wait, 0)
    lax.fori_loop(1, ne, res_start, 0)
    for copy in locals_:
        copy.wait()
    for copy in mix_far + mix_near + mix_relay:
        copy.wait_send()
    if not roomy:
        load = pltpu.make_async_copy(back, got, here.at[0])
        load.start()
        load.wait()
    rows_back = back if roomy else got
    slots = n * block
    grad_s, gg_s, tok_s = cot_pad, gall, mall

    def hot(q):
        s = iota((1, slots), 1)
        c = slotc[q]
        return ((c[:, 0:1] == s) | (c[:, 1:2] == s)).astype(f32).astype(bf16)

    def grad_tokens(q):
        grad_s[q] = dot(hot(q), rows_back[...].reshape(slots, width)).astype(bf16)

    def gate_tokens(q):
        sc = iota((slots, 1), 0)
        gg_s[q] = jnp.zeros(gg_s.shape[1:], f32)
        for k in range(TOP):
            gg_s[q, k : k + 1, :] = jnp.sum(
                jnp.where(slotr[q, k : k + 1, :] == sc, gate_s[0:slots, :], 0.0), axis=0, keepdims=True
            )

    stages = ((grad_s, tin1, keep_g, tin2), (gg_s, tin1k, keep_k, tin2k))
    first = {}
    for i, (src, dst, _, _) in enumerate(stages):
        if i == 1:


            def read_gates(d, carry):
                gr = rows_back[d, block - 2 : block - 1, 0:block].astype(f32)
                gr = gr + rows_back[d, block - 1 : block, 0:block].astype(f32)
                gate_s[pl.ds(pl.multiple_of(d * block, block), block), :] = to_col(gr)
                return carry

            lax.fori_loop(0, n, read_gates, 0)
        for j, q in enumerate((cross, near)):
            (grad_tokens, gate_tokens)[i](q)
            k = 3 * i + j
            first[i, j] = remote(src.at[q], dst.at[j], usend.at[k], urecv.at[k], (e, near))
            first[i, j].start()
        (grad_tokens, gate_tokens)[i](far)
    second = []
    for i, (src, one, held, two) in enumerate(stages):
        first[i, 0].wait()
        held[...] = (src[far].astype(f32) + one[0].astype(f32)).astype(held.dtype)
        copy = remote(held, two, usend.at[3 * i + 2], urecv.at[3 * i + 2], (e, far))
        copy.start()
        second.append(copy)
    grad_tokens(t)
    gate_tokens(t)
    ebuf[...] = g_result()
    e_first = sum_copy(ne, ebuf, eparts, esend, erecv)
    start_all(ne, e_first)
    unit2, scale2 = norm_stats(middle[...])
    sums = []
    for i, (src, one, _, two) in enumerate(stages):
        first[i, 1].wait()
        mine = src[t].astype(f32) + one[1].astype(f32)
        second[i].wait()
        sums.append(mine + two[...].astype(f32))
    gmix, ggate = sums
    gg0 = to_col(ggate[0:1, :])
    gg1 = to_col(ggate[1:2, :])
    inner = prob0 * gg0 + prob1 * gg1
    lane = iota((1, rw.shape[0]), 1)
    glog = jnp.where(r[:, 0:1] == lane, prob0 * (gg0 - inner), 0.0) + jnp.where(
        r[:, 1:2] == lane, prob1 * (gg1 - inner), 0.0
    )
    llow = dot_fine(glog, ru[...]) * pick
    gm = gmix + dot_fine(glog, rw[...]) + dot_nt_fine(llow, rd[...])
    router_up = dot_tn(glog.astype(bf16), rlow.astype(bf16))
    router_down = dot_tn(mixed[...], llow.astype(bf16))
    gmid = cot_own[...].astype(f32) + norm_back(gm, gain2[...], unit2, scale2)
    mid_at, in_at = pl.ds(0, rows), pl.ds(rows, rows)
    acc_s[mid_at, :] = gmid
    gbranch = gmid.astype(bf16)
    project_up = dot_tn(plow[...], gbranch)
    blow = (dot_nt(gbranch, pup[...]) * pick).astype(bf16)
    for p in range(nt):
        ga_s[p] = (dot_nt(gbranch, pw[p]) + dot_nt(blow, pd[p])).astype(bf16)

    for q in range(nt):
        off = la
        at = slice(q * share, (q + 1) * share)
        for c in range(width // 128):
            gr_s[q, off : off + share, :] = project_up[at, c * 128 : (c + 1) * 128].astype(bf16)
            off += share
        at = slice(q * quarter, (q + 1) * quarter)
        gr_s[q, off : off + quarter, :] = router_down[at].astype(bf16)
        off += quarter
        gr_s[q, off : la + lb - lw, :] = jnp.zeros((la + lb - lw - off, 128), bf16)
        gr_s[q, la + lb - lw : la + lb, :] = dot_tn(attended[q], blow).astype(bf16)
    off = la + ADAPT + quarter
    gr_s[0, off : off + experts, :] = router_up.astype(bf16)
    b_start, b_cross, b_result = tensor_sum(pl.ds(la, lb), bin1, bin2, 3)
    b_start()
    b_first = sum_copy(ne, bbuf, bparts, b2send, b2recv)

    acc_s[in_at, :] = jnp.zeros((rows, width), f32)
    back_low[...] = jnp.zeros_like(back_low)

    def piece_back(p, carry):
        for li in range(per):
            at = pl.ds(li * seqp, seqp)
            q = triple[p, at, 0:lw]
            k = triple[p, at, lw : 2 * lw]
            v = triple[p, at, 2 * lw : 3 * lw]
            ga = ga_s[p, at, :]
            gq = jnp.zeros((seqp, lw), f32)
            gk = jnp.zeros((seqp, lw), f32)
            gv = jnp.zeros((seqp, lw), f32)
            for h in range(lw // HEAD_DIM):
                on = head_of == h
                qm = jnp.where(on, q, 0.0).astype(bf16)
                km = jnp.where(on, k, 0.0).astype(bf16)
                gam = jnp.where(on, ga, 0.0).astype(bf16)
                probs = softmax_of(qm, k)
                gp = dot_nt(gam, v)
                ds = (probs * (gp - jnp.sum(probs * gp, axis=1, keepdims=True))).astype(bf16)
                gq = gq + dot(ds, km)
                gk = gk + dot_tn(ds, qm)
                gv = gv + dot_tn(probs.astype(bf16), gam)
            gt_s[at, 0:lw] = (gq * HEAD_DIM**-0.5).astype(bf16)
            gt_s[at, lw : 2 * lw] = (gk * HEAD_DIM**-0.5).astype(bf16)
            gt_s[at, 2 * lw : 3 * lw] = gv.astype(bf16)
        gt = gt_s[...]
        back_low[...] += dot_nt(gt, tup[p])
        acc_s[in_at, :] += dot_nt(gt, wt[p])
        tu = dot_tn(tlow[...], gt)
        for c in range(3 * lw // 128):
            gr_s[p, c * 128 : (c + 1) * 128, :] = tu[:, c * 128 : (c + 1) * 128].astype(bf16)

        @pl.when(p == 0)
        def _():
            b_cross()

        @pl.when(p == 2)
        def _():
            bbuf[...] = b_result()
            start_all(ne, b_first)

        return carry

    lax.fori_loop(0, nt, piece_back, 0)

    tglow = (back_low[...] * pick).astype(bf16)
    triple_down = dot_tn(attn_in[...], tglow)
    for q in range(nt):
        off = 3 * lw
        gr_s[q, off : off + quarter, :] = triple_down[q * quarter : (q + 1) * quarter].astype(bf16)
        if off + quarter < la:
            gr_s[q, off + quarter : la, :] = jnp.zeros((la - off - quarter, 128), bf16)
    a_start, a_cross, a_result = tensor_sum(pl.ds(0, la), ain1, ain2, 6)
    a_start()
    gin = acc_s[in_at, :] + dot_nt(tglow, tdn[...])
    a_cross()
    unit1, scale1 = norm_stats(xs[...])
    attn_in[...] = (acc_s[mid_at, :] + norm_back(gin, gain1[...], unit1, scale1)).astype(bf16)

    def share_out(j, src, k):
        return [
            remote(src, outs.at[t, j], osend.at[k], orecv.at[k], (e, far)),
            remote(src, outs.at[t, j], osend.at[k + 1], orecv.at[k + 1], (e, near)),
            remote(outs.at[far, j], outs.at[far, j], osend.at[k + 2], orecv.at[k + 2], (e, near)),
            pltpu.make_async_copy(src, outs.at[t, j], here.at[1 + j]),
        ]

    def share_rows(buf, k):
        return [
            remote(buf.at[t], buf.at[t], osend.at[k], orecv.at[k], (e, far)),
            remote(buf.at[t], buf.at[t], osend.at[k + 1], orecv.at[k + 1], (e, near)),
            remote(buf.at[far], buf.at[far], osend.at[k + 2], orecv.at[k + 2], (e, near)),
        ]

    igrad_out = share_out(1, attn_in, 0)
    for i in (0, 1, 3):
        igrad_out[i].start()
    def res_wait(d, carry):
        res_copy(d).wait()
        return carry

    lax.fori_loop(1, ne, res_wait, 0)
    if not roomy:
        load = pltpu.make_async_copy(got_res, got_cot, here.at[0])
        load.start()
        load.wait()
    res_rows = got_res if roomy else got_cot

    def res_tokens(q):
        tok_s[q] = dot(hot(q), res_rows[...].reshape(slots, width)).astype(bf16)

    res_first = []
    for j, q in enumerate((cross, near)):
        res_tokens(q)
        res_first.append(remote(tok_s.at[q], tin1r.at[j], usend.at[6 + j], urecv.at[6 + j], (e, near)))
        res_first[-1].start()
    res_tokens(far)
    res_first[0].wait()
    keep_g[...] = (tok_s[far].astype(f32) + tin1r[0].astype(f32)).astype(bf16)
    res_second = remote(keep_g, tin2r, usend.at[8], urecv.at[8], (e, far))
    res_second.start()
    res_tokens(t)
    abuf = keep.at[pl.ds(la, la)]
    abuf[...] = a_result()
    a_first = sum_copy(ne, abuf, aparts, asend, arecv)
    start_all(ne, a_first)
    e_second = sum_share(ne, e_first, ebuf, eparts, etot, esend, erecv)
    b_second = sum_share(ne, b_first, bbuf, bparts, btot, b2send, b2recv)
    a_second = sum_share(ne, a_first, abuf, aparts, atot, asend, arecv)
    wait_all(ne, e_second)
    wait_all(ne, b_second)
    ra = grows - held_e
    rep_e[t, 0:ra, :] = etot[held_e:grows, :]
    rep_e[t, ra:, :] = btot[0 : lb - lw, :]
    rep_out = share_rows(rep_e, 6)
    for i in (0, 1):
        rep_out[i].start()
    wait_all(ne, a_second)
    rep_a[t] = atot[3 * lw : 3 * lw + quarter, :]
    last_out = share_rows(rep_a, 9)
    for i in (0, 1):
        last_out[i].start()
    res_first[1].wait()
    res_second.wait()
    mixed[...] = (
        middle[...] + (tok_s[t].astype(f32) + tin1r[1].astype(f32)) + tin2r[...].astype(f32)
    ).astype(bf16)
    block_out = share_out(0, mixed, 3)
    for i in (0, 1, 3):
        block_out[i].start()
    igrad_out[0].wait_recv()
    igrad_out[2].start()
    for group in (block_out, rep_out, last_out):
        group[0].wait_recv()
        group[2].start()
    for group in (igrad_out, block_out, rep_out, last_out):
        group[0].wait_send()
        for copy in group[1:]:
            copy.wait()
    for copy in fars + relays + big_far + big_relay:
        copy.wait_send()


def write_kernel(
    dims, e_all, b_all, a_all, outs, rep_e, rep_a, block_output, input_grad, triple_down, triple_up, project_down,
    project_up, router_down, router_up, first_down, first_up, second_down, second_up,
):
    nt, seq, seqp, images, ffq, lw, grows = dims
    per = images // nt
    tok, width = block_output.shape
    flat = outs.shape[2]
    for j, out in enumerate((block_output, input_grad)):
        for a in range(0, tok, seqp):
            b = min(a + seqp, tok)
            i0, i1 = a // seq, (b - 1) // seq
            parts = []
            for i in range(i0, i1 + 1):
                row = iota((b - a, seqp), 0) + a
                sel = (iota((b - a, seqp), 1) == row - i * seq) & (row < (i + 1) * seq)
                src = outs[i // per, j, (i % per) * seqp : (i % per + 1) * seqp, :]
                parts.append(dot(sel.astype(f32).astype(bf16), src))
            whole_part = parts[0]
            for part in parts[1:]:
                whole_part = whole_part + part
            out[a:b, :] = whole_part.astype(bf16)
    for c in range(ffq // 128):
        first_up[:, c * 128 : (c + 1) * 128] = e_all[c * 128 : (c + 1) * 128].astype(f32)
    second_down[...] = e_all[ffq : 2 * ffq].astype(f32)
    for c in range(3):
        triple_up[c] = a_all[c * lw : (c + 1) * lw].astype(f32)
    last = b_all.shape[0]
    project_down[...] = b_all[last - lw : last].astype(f32)
    quarter = width // nt
    share = ADAPT // nt
    for q in range(nt):
        at = slice(q * quarter, (q + 1) * quarter)
        up_at = slice(q * share, (q + 1) * share)
        triple_down[at, :] = rep_a[q].astype(f32)
        first_down[at, :] = rep_e[q, 0:quarter, :].astype(f32)
        off = quarter
        for c in range(width // 128):
            second_up[up_at, c * 128 : (c + 1) * 128] = rep_e[q, off : off + share, :].astype(f32)
            off += share
        off = grows - 2 * ffq
        for c in range(width // 128):
            project_up[up_at, c * 128 : (c + 1) * 128] = rep_e[q, off : off + share, :].astype(f32)
            off += share
        router_down[at, :] = rep_e[q, off : off + quarter, :].astype(f32)
        off += quarter
    router_up[...] = rep_e[0, off : off + router_up.shape[0], :].astype(f32)


def body(
    inputs, gain_attend, triple_weight, project_weight, gain_mixture, router_weight, expert_first,
    expert_second, triple_down, triple_up, project_down, project_up, router_down, router_up,
    first_down, first_up, second_down, second_up, adapter_index, routes, priority, cotangent,
):
    ne = lax.axis_size("expert")
    nt = lax.axis_size("tensor")
    tok, width = inputs.shape
    images = adapter_index.shape[0]
    seq = tok // images
    seqp = up(seq, 16)
    per = images // nt
    rows = per * seqp
    experts = router_weight.shape[1]
    local = expert_first.shape[0]
    ffq = expert_first.shape[2]
    lw = triple_weight.shape[2]
    cap = nt * ((5 * tok * TOP + 4 * nt * experts - 1) // (4 * nt * experts))
    used = cap * local // nt
    chunks = 2
    block = up(used + 4, 16 * chunks)
    cp = block // chunks
    smem = pl.BlockSpec(memory_space=pltpu.SMEM)
    anywhere = pl.BlockSpec(memory_space=pl.ANY)
    shape = jax.ShapeDtypeStruct
    wide = up(2 * experts, 128)
    gain1 = gain_attend.reshape(1, width)
    gain2 = gain_mixture.reshape(1, width)
    rw = router_weight.T
    ru = router_up.T
    big = (expert_first, expert_second, first_up, second_down)
    n_w = 8
    erows = ne * cp
    quarter = width // nt
    held_e = 2 * ffq
    grows = up(held_e + quarter + (ADAPT // nt) * (width // 128), 16 * ne)
    one = (rows, width)
    small = (8, rows)
    la = up(3 * lw + quarter, 16 * ne)
    lb = up(ADAPT + quarter + experts + lw, 16 * ne)
    re = grows + lb - lw - held_e
    n_big = len(big)
    slots = (ne, block, width)
    roomy = ne * block <= 1024
    spare = slots if roomy else (8, 128)
    finals = pl.pallas_call(
        functools.partial(
            block_kernel,
            (nt, ne, seq, seqp, images, experts, cap, chunks, cp, held_e, grows, la, lb, roomy),
        ),
        out_shape=[
            shape((grows, 128), bf16),
            shape((lb, 128), bf16),
            shape((la, 128), bf16),
            shape((nt, 2) + one, bf16),
            shape((nt, re, 128), bf16),
            shape((nt, quarter, 128), bf16),
            shape((8, 128) if roomy else slots, bf16),
            shape((8, 128) if roomy else slots, bf16),
        ],
        in_specs=[smem] + whole(2) + [anywhere] * 2 + whole(13) + [anywhere] * 4,
        out_specs=whole(3) + [anywhere] + whole(2) + [anywhere] * 2,
        scratch_shapes=[
            VMEM((nt, rows, TOP), i32),
            VMEM((nt, TOP, rows), i32),
            VMEM((nt, rows, TOP), i32),
            VMEM(one, f32),
            VMEM(one, bf16),
            VMEM(one, bf16),
            VMEM(one, f32),
            VMEM((nt, rows, 3 * lw), bf16),
            VMEM((nt, rows, lw), bf16),
            VMEM((rows, ADAPT), bf16),
            VMEM((rows, ADAPT), bf16),
            VMEM(one, bf16),
            VMEM((nt, width, 3 * lw), bf16),
            VMEM((nt, ADAPT, 3 * lw), bf16),
            VMEM((nt, lw, width), bf16),
            VMEM((nt, lw, ADAPT), bf16),
            VMEM(slots, bf16),
            VMEM(slots, bf16),
            VMEM((nt,) + one, bf16),
            VMEM((images * seqp, wide), bf16),
            VMEM(slots, bf16),
            VMEM((nt,) + one, bf16),
            VMEM((nt,) + small, f32),
            VMEM((max(ne * block, 2 * erows, 2 * rows), width), f32),
            VMEM((max(ne * block, images * seqp), 1), f32),
            VMEM(slots, bf16),
            VMEM((nt, width, ffq), bf16),
            VMEM((nt, ffq, width), bf16),
            VMEM((nt, ADAPT, ffq), bf16),
            VMEM((nt, ffq, ADAPT), bf16),
            VMEM((erows, width), bf16),
            VMEM((erows, width), bf16),
            VMEM((2, erows, ADAPT), bf16),
            VMEM((ne, block, 2), f32),
            VMEM((ne, block), f32),
            VMEM((2, erows, ADAPT), f32),
            VMEM((ADAPT, width), f32),
            VMEM((nt, ADAPT, ffq), f32),
            VMEM((nt, ADAPT, ffq), f32),
            VMEM((ADAPT, width), f32),
            VMEM((nt, max(grows, la + lb), 128), bf16),
            VMEM((2, grows, 128), bf16),
            VMEM((max(grows, la + lb, 2 * la), 128), bf16),
            VMEM((grows, 128), bf16),
            VMEM((tok, width), bf16),
            VMEM((tok, width) if roomy else (8, 128), bf16),
            VMEM(spare, bf16),
            VMEM(spare, bf16),
            VMEM((2,) + one, bf16),
            VMEM((2,) + small, f32),
            VMEM((2,) + one, bf16),
            VMEM(one, bf16),
            VMEM(small, f32),
            VMEM(one, bf16),
            VMEM(small, f32),
            VMEM(one, bf16),
            VMEM((2, lb, 128), bf16),
            VMEM((lb, 128), bf16),
            VMEM((2, la, 128), bf16),
            VMEM((la, 128), bf16),
            VMEM((ne - 1, grows // ne, 128), bf16),
            VMEM((ne - 1, lb // ne, 128), bf16),
            VMEM((ne - 1, la // ne, 128), bf16),
            VMEM((rows, 3 * lw), bf16),
            VMEM((nt, rows, lw), bf16),
            VMEM((rows, ADAPT), f32),
            VMEM((nt, rows), f32),
            dma(3 * n_w),
            dma(3 * n_w),
            dma(3 * n_big),
            dma(3 * n_big),
            dma(ne),
            dma(ne),
            dma(6),
            dma(6),
            dma(chunks * ne),
            dma(chunks * ne),
            dma(chunks * ne),
            dma(chunks * ne),
            dma(ne),
            dma(ne),
            dma(9),
            dma(9),
            dma(9),
            dma(9),
            dma(2 * ne),
            dma(2 * ne),
            dma(2 * ne),
            dma(2 * ne),
            dma(2 * ne),
            dma(2 * ne),
            dma(12),
            dma(12),
            dma(3),
            dma(n_w),
            dma(n_big + 2),
            dma(2),
        ],
        compiler_params=pltpu.CompilerParams(
            collective_id=0, has_side_effects=True, vmem_limit_bytes=67000000
        ),
        name="block",
    )(
        adapter_index, priority, routes.T, cotangent, inputs, gain1, gain2,
        triple_weight.transpose(1, 0, 2), triple_up.transpose(1, 0, 2), project_weight,
        project_down, triple_down, project_up, rw, router_down, ru, first_down, second_up, *big,
    )

    outs = pl.pallas_call(
        functools.partial(write_kernel, (nt, seq, seqp, images, ffq, lw, grows)),
        out_shape=[
            shape((tok, width), bf16),
            shape((tok, width), bf16),
            shape((width, ADAPT), f32),
            shape((3, ADAPT, lw), f32),
            shape((lw, ADAPT), f32),
            shape((ADAPT, width), f32),
            shape((width, ADAPT), f32),
            shape((experts, ADAPT), f32),
            shape((width, ADAPT), f32),
            shape((ADAPT, ffq), f32),
            shape((ffq, ADAPT), f32),
            shape((ADAPT, width), f32),
        ],
        in_specs=whole(6),
        out_specs=whole(12),
        name="write",
    )(*finals[:6])
    outs = list(outs)
    outs[3] = outs[3].transpose(1, 0, 2)
    outs[7] = outs[7].T
    return tuple(outs)


def solution(mesh):
    return jax.shard_map(
        body,
        mesh=mesh,
        in_specs=(
            P("expert", None),
            P(),
            P(None, None, "tensor"),
            P("tensor", None),
            P(),
            P(),
            P("expert", None, "tensor"),
            P("expert", "tensor", None),
            P(),
            P(None, None, "tensor"),
            P("tensor", None),
            P(),
            P(),
            P(),
            P(),
            P(None, "tensor"),
            P("tensor", None),
            P(),
            P("expert"),
            P("expert", None),
            P("expert", None),
            P("expert", None),
        ),
        out_specs=(
            P("expert", None),
            P("expert", None),
            P(),
            P(None, None, "tensor"),
            P("tensor", None),
            P(),
            P(),
            P(),
            P(),
            P(None, "tensor"),
            P("tensor", None),
            P(),
        ),
        check_vma=False,
    )
```

profile of v0, /device:TPU:31, one launch (start us, length us, event | category | flops | bytes accessed | tf_op | source)
XLA Modules:
  0.0 172.9 jit_solution(10290534200260128429)
XLA Ops:
  0.7 166.3 %block.1 = (bf16[1280,128]{1,0:T(8,128)(2,1)}, bf16[512,128]{1,0:T(8,128)(2,1)}, bf16[512,128]{1,0:T(8,128)(2,1)}, bf16[4,2,416,512]{3,2,1,0:T(8,128)(2,1)}, bf1...) custom-call(s32[8]{0:T(128)} %adapters.1, ...), custom_call_target="tpu_custom_call" | custom-call | tf_op jit(solution)/shard_map/block/pallas_call | solution.py:1140
  167.0 5.9 %write.1 = (bf16[1576,512]{1,0:T(8,128)(2,1)}, bf16[1576,512]{1,0:T(8,128)(2,1)}, f32[512,128]{1,0:T(8,128)}, f32[3,128,128]{2,1,0:T(8,128)}, f32[128,128]{1,0:T...) custom-call(bf16[1280,128]{1,0:T(8,128)(2,1)} %get-tuple-element.30., ...), custom_call_target="tpu_custom_call" | custom-call | tf_op jit(solution)/shard_map/write/pallas_call | solution.py:1266
where the time goes:
time: 174 us; the launch traced here: 173 us
  Pallas kernels  172 us (99%)
    pallas_call x1, Pallas kernels, body(): pl.pallas_call(functools.partial(block_kernel, (nt, ne, seq, seqp, images...  166 us
    pallas_call x1, Pallas kernels, body(): pl.pallas_call(functools.partial(write_kernel, (nt, seq, seqp, images, ff...  5.86 us

commit v1 on v0

--- a/solution.py
+++ b/solution.py
@@ -208,7 +208,7 @@
         w1, w2, fup, sdn, sent_s, sg_s, low_s, gcol_s, gg_rows, acc_low,
         acc_fd, acc_fu, acc_sd, acc_su, gr_s, gin1, keep, gin2, cot, x_own,
         back_s, res_s, tin1, tin1k, tin1r, keep_g, keep_k, tin2, tin2k, tin2r,
-        bin1, bin2, ain1, ain2, eparts, bparts, aparts, gt_s, ga_s, back_low, rank_r,
+        bin1, bin2, ain1, ain2, eparts, bparts, aparts, gt_s, ga_s, back_low, rank_r, probs_s,
         wsend, wrecv, bsend, brecv, csend, crecv, tsend, trecv, send, recv, gsend, grecv, rsend, rrecv,
         ssend, srecv, usend, urecv, esend, erecv, b2send, b2recv, asend, arecv, osend, orecv,
         here, own_sem, load_sem, ret_sem,
@@ -448,10 +448,10 @@
             acc = jnp.zeros((seqp, lw), f32)
             for h in range(lw // HEAD_DIM):
                 on = head_of == h
-                s = dot_nt(jnp.where(on, q, 0.0).astype(bf16), k) * HEAD_DIM**-0.5
-                s = jnp.where(key_ok, s, -jnp.inf)
+                qm = jnp.where(on, q * HEAD_DIM**-0.5, 0.0).astype(bf16)
+                s = jnp.where(key_ok, dot_nt(qm, k), -jnp.inf)
                 ex = jnp.exp(s - jnp.max(s, axis=1, keepdims=True))
-                probs = (ex / jnp.sum(ex, axis=1, keepdims=True)).astype(bf16)
+                probs = (ex * (1.0 / jnp.sum(ex, axis=1, keepdims=True))).astype(bf16)
                 acc = acc + dot(probs, jnp.where(on, v, 0.0).astype(bf16))
             attended[p, at, :] = acc.astype(bf16)
         return carry
@@ -782,10 +782,26 @@
     )
     g_cross()
 
+    key_row = iota((seqp, 1), 0) < seq
+    heads = lw // HEAD_DIM
+
     def softmax_of(qm, k):
-        s = jnp.where(key_ok, dot_nt(qm, k) * HEAD_DIM**-0.5, -jnp.inf)
-        ex = jnp.exp(s - jnp.max(s, axis=1, keepdims=True))
-        return ex / jnp.sum(ex, axis=1, keepdims=True)
+        s = jnp.where(key_row, dot_nt(k, qm), -jnp.inf)
+        ex = jnp.exp(s - jnp.max(s, axis=0, keepdims=True))
+        return ex * (1.0 / jnp.sum(ex, axis=0, keepdims=True))
+
+    def softmax_piece(p, carry):
+        for li in range(per):
+            at = pl.ds(li * seqp, seqp)
+            q = triple[p, at, 0:lw] * HEAD_DIM**-0.5
+            k = triple[p, at, lw : 2 * lw]
+            for h in range(heads):
+                qm = jnp.where(head_of == h, q, 0.0).astype(bf16)
+                probs_s[(p * per + li) * heads + h] = softmax_of(qm, k).astype(bf16)
+        return carry
+
+    if roomy:
+        lax.fori_loop(0, nt, softmax_piece, 0)
 
     def back_wait(d, carry):
         for h in range(chunks):
@@ -823,8 +839,8 @@
             )
 
     stages = ((grad_s, tin1, keep_g, tin2), (gg_s, tin1k, keep_k, tin2k))
-    first = {}
-    for i, (src, dst, _, _) in enumerate(stages):
+    first, second = {}, []
+    for i, (src, dst, held, two) in enumerate(stages):
         if i == 1:
 
 
@@ -841,13 +857,10 @@
             first[i, j] = remote(src.at[q], dst.at[j], usend.at[k], urecv.at[k], (e, near))
             first[i, j].start()
         (grad_tokens, gate_tokens)[i](far)
-    second = []
-    for i, (src, one, held, two) in enumerate(stages):
         first[i, 0].wait()
-        held[...] = (src[far].astype(f32) + one[0].astype(f32)).astype(held.dtype)
-        copy = remote(held, two, usend.at[3 * i + 2], urecv.at[3 * i + 2], (e, far))
-        copy.start()
-        second.append(copy)
+        held[...] = (src[far].astype(f32) + dst[0].astype(f32)).astype(held.dtype)
+        second.append(remote(held, two, usend.at[3 * i + 2], urecv.at[3 * i + 2], (e, far)))
+        second[-1].start()
     grad_tokens(t)
     gate_tokens(t)
     ebuf[...] = g_result()
@@ -904,26 +917,31 @@
     def piece_back(p, carry):
         for li in range(per):
             at = pl.ds(li * seqp, seqp)
-            q = triple[p, at, 0:lw]
+            q = triple[p, at, 0:lw] * HEAD_DIM**-0.5
             k = triple[p, at, lw : 2 * lw]
             v = triple[p, at, 2 * lw : 3 * lw]
             ga = ga_s[p, at, :]
             gq = jnp.zeros((seqp, lw), f32)
             gk = jnp.zeros((seqp, lw), f32)
             gv = jnp.zeros((seqp, lw), f32)
-            for h in range(lw // HEAD_DIM):
+            for h in range(heads):
                 on = head_of == h
                 qm = jnp.where(on, q, 0.0).astype(bf16)
                 km = jnp.where(on, k, 0.0).astype(bf16)
                 gam = jnp.where(on, ga, 0.0).astype(bf16)
-                probs = softmax_of(qm, k)
-                gp = dot_nt(gam, v)
-                ds = (probs * (gp - jnp.sum(probs * gp, axis=1, keepdims=True))).astype(bf16)
-                gq = gq + dot(ds, km)
-                gk = gk + dot_tn(ds, qm)
-                gv = gv + dot_tn(probs.astype(bf16), gam)
+                if roomy:
+                    half = probs_s[(p * per + li) * heads + h]
+                    probs = half.astype(f32)
+                else:
+                    probs = softmax_of(qm, k)
+                    half = probs.astype(bf16)
+                weighted = probs * dot_nt(v, gam)
+                ds = (weighted - probs * jnp.sum(weighted, axis=0, keepdims=True)).astype(bf16)
+                gq = gq + dot_tn(ds, km)
+                gk = gk + dot(ds, qm)
+                gv = gv + dot(half, gam)
             gt_s[at, 0:lw] = (gq * HEAD_DIM**-0.5).astype(bf16)
-            gt_s[at, lw : 2 * lw] = (gk * HEAD_DIM**-0.5).astype(bf16)
+            gt_s[at, lw : 2 * lw] = gk.astype(bf16)
             gt_s[at, 2 * lw : 3 * lw] = gv.astype(bf16)
         gt = gt_s[...]
         back_low[...] += dot_nt(gt, tup[p])
@@ -1013,7 +1031,7 @@
     wait_all(ne, b_second)
     ra = grows - held_e
     rep_e[t, 0:ra, :] = etot[held_e:grows, :]
-    rep_e[t, ra:, :] = btot[0 : lb - lw, :]
+    rep_e[t, ra:, :] = btot[0 : rep_e.shape[1] - ra, :]
     rep_out = share_rows(rep_e, 6)
     for i in (0, 1):
         rep_out[i].start()
@@ -1132,7 +1150,7 @@
     small = (8, rows)
     la = up(3 * lw + quarter, 16 * ne)
     lb = up(ADAPT + quarter + experts + lw, 16 * ne)
-    re = grows + lb - lw - held_e
+    re = grows - held_e + ADAPT + quarter + experts
     n_big = len(big)
     slots = (ne, block, width)
     roomy = ne * block <= 1024
@@ -1222,6 +1240,7 @@
             VMEM((nt, rows, lw), bf16),
             VMEM((rows, ADAPT), f32),
             VMEM((nt, rows), f32),
+            VMEM((nt * per * lw // HEAD_DIM, seqp, seqp) if roomy else (1, 16, 128), bf16),
             dma(3 * n_w),
             dma(3 * n_w),
             dma(3 * n_big),

time: 174 us -> 170 us (0.977)
  Pallas kernels: 172 us -> 168 us
    pallas_call x1, Pallas kernels: 166 us -> 163 us  [body(): pl.pallas_call(functools.partial(block_kernel, (nt, ne, seq, seqp, images...]
where the time goes in v1:
time: 170 us; the launch traced here: 169 us
  Pallas kernels  168 us (99%)
    pallas_call x1, Pallas kernels, body(): pl.pallas_call(functools.partial(block_kernel, (nt, ne, seq, seqp, images...  163 us
    pallas_call x1, Pallas kernels, body(): pl.pallas_call(functools.partial(write_kernel, (nt, seq, seqp, images, ff...  5.82 us

profile of v1, /device:TPU:31, one launch (start us, length us, event | category | flops | bytes accessed | tf_op | source)
XLA Modules:
  0.0 169.1 jit_solution(14342505804602954406)
XLA Ops:
  0.7 162.6 %block.1 = (bf16[1280,128]{1,0:T(8,128)(2,1)}, bf16[512,128]{1,0:T(8,128)(2,1)}, bf16[512,128]{1,0:T(8,128)(2,1)}, bf16[4,2,416,512]{3,2,1,0:T(8,128)(2,1)}, bf1...) custom-call(s32[8]{0:T(128)} %adapters.1, ...), custom_call_target="tpu_custom_call" | custom-call | tf_op jit(solution)/shard_map/block/pallas_call | solution.py:1158
  163.3 5.8 %write.1 = (bf16[1576,512]{1,0:T(8,128)(2,1)}, bf16[1576,512]{1,0:T(8,128)(2,1)}, f32[512,128]{1,0:T(8,128)}, f32[3,128,128]{2,1,0:T(8,128)}, f32[128,128]{1,0:T...) custom-call(bf16[1280,128]{1,0:T(8,128)(2,1)} %get-tuple-element.30., ...), custom_call_target="tpu_custom_call" | custom-call | tf_op jit(solution)/shard_map/write/pallas_call | solution.py:1285

commit v2 on v1

--- a/solution.py
+++ b/solution.py
@@ -152,7 +152,7 @@
     e, t = where_am_i()[:2]
 
     def copy(d):
-        p = lax.rem(e + d, ne)
+        p = lax.rem(e + 3 * d, ne)
         return remote(src.at[chunk_of(src, ne, p)], parts.at[d - 1], send.at[d], recv.at[d], (p, t))
 
     return copy
@@ -177,7 +177,7 @@
     total[mine, :] = lax.fori_loop(1, ne, add, src[mine, :].astype(f32)).astype(bf16)
 
     def share(d):
-        p = lax.rem(e + d, ne)
+        p = lax.rem(e + 3 * d, ne)
         return remote(total.at[mine], total.at[mine], send.at[ne + d], recv.at[ne + d], (p, t))
 
     def start(d, carry):
@@ -222,7 +222,7 @@
     local = w1_in.shape[0]
     parts = nt // local
     n_out, block = cots.shape[0], cots.shape[1]
-    peers = [(e, far), (e, near)] + [(lax.rem(e + d, ne), t) for d in range(1, ne)]
+    peers = [(e, far), (e, near)] + [(lax.rem(e + 3 * d, ne), t) for d in range(1, ne)]
     barrier = pltpu.get_barrier_semaphore()
     for peer in peers:
         pl.semaphore_signal(barrier, 1, device_id=peer, device_id_type=MESH)
@@ -384,7 +384,7 @@
     lax.fori_loop(0, n_out // step, pack, 0)
 
     def cot_copy(d):
-        p = lax.rem(e + d, ne)
+        p = lax.rem(e + 3 * d, ne)
         return remote(cots.at[p], got_cot.at[e], csend.at[d], crecv.at[d], (p, t))
 
     def cot_start(d, carry):
@@ -549,12 +549,12 @@
         return pl.ds(pl.multiple_of(h * cp, cp), cp)
 
     def out_copy(d, h):
-        p = lax.rem(e + d, ne)
+        p = lax.rem(e + 3 * d, ne)
         k = d * chunks + h
         return remote(out_s.at[p, chunk(h)], got.at[e, chunk(h)], send.at[k], recv.at[k], (p, t))
 
     def send_one(d, carry):
-        p = lax.rem(e + d, ne)
+        p = lax.rem(e + 3 * d, ne)
         head, tail = finish(p)
         out_s[p, :, 0:block] = head
         out_s[p, :, block:] = tail
@@ -591,12 +591,12 @@
     own_cot.wait()
 
     def grad_copy(d, h):
-        p = lax.rem(e + d, ne)
+        p = lax.rem(e + 3 * d, ne)
         k = d * chunks + h
         return remote(cots.at[p, chunk(h)], back.at[e, chunk(h)], gsend.at[k], grecv.at[k], (p, t))
 
     def res_copy(d):
-        p = lax.rem(e + d, ne)
+        p = lax.rem(e + 3 * d, ne)
         return remote(out_s.at[p], got_res.at[e], rsend.at[d], rrecv.at[d], (p, t))
 
     def experts_chunk(h, carry):

time: 170 us -> 171 us (level)
  no operation moved by 1% of the time
where the time goes in v2:
time: 171 us; the launch traced here: 169 us
  Pallas kernels  168 us (98%)
    pallas_call x1, Pallas kernels, body(): pl.pallas_call(functools.partial(block_kernel, (nt, ne, seq, seqp, images...  162 us
    pallas_call x1, Pallas kernels, body(): pl.pallas_call(functools.partial(write_kernel, (nt, seq, seqp, images, ff...  5.82 us

profile of v2, /device:TPU:31, one launch (start us, length us, event | category | flops | bytes accessed | tf_op | source)
XLA Modules:
  0.0 168.6 jit_solution(9511308471178188810)
XLA Ops:
  0.7 162.1 %block.1 = (bf16[1280,128]{1,0:T(8,128)(2,1)}, bf16[512,128]{1,0:T(8,128)(2,1)}, bf16[512,128]{1,0:T(8,128)(2,1)}, bf16[4,2,416,512]{3,2,1,0:T(8,128)(2,1)}, bf1...) custom-call(s32[8]{0:T(128)} %adapters.1, ...), custom_call_target="tpu_custom_call" | custom-call | tf_op jit(solution)/shard_map/block/pallas_call | solution.py:1158
  162.8 5.8 %write.1 = (bf16[1576,512]{1,0:T(8,128)(2,1)}, bf16[1576,512]{1,0:T(8,128)(2,1)}, f32[512,128]{1,0:T(8,128)}, f32[3,128,128]{2,1,0:T(8,128)}, f32[128,128]{1,0:T...) custom-call(bf16[1280,128]{1,0:T(8,128)(2,1)} %get-tuple-element.30., ...), custom_call_target="tpu_custom_call" | custom-call | tf_op jit(solution)/shard_map/write/pallas_call | solution.py:1285
